TPU v7x, 512 devices: a whole 4x4x16 slice. The times are simulated.
512 devices in a mesh: rows: 128 (over x, z, core), rhs: 4 (over y).
Axes of the slice: x: 4, y: 4, z: 16, core: 2. Of those that a mesh axis runs over, the one named last changes fastest.
Arguments:
- targets: float32 [32768, 1024], P(('rows', 'rhs')), may hold values from -6 to 6
- send_order: int32 [32768], P('rows'), may hold values from 0 to 255, as said below
- send_count: int32 [128, 128], P('rows'), may hold values from 0 to 4, as said below
- recv_slot: int32 [32768], P('rows'), may hold values from 0 to 255, as said below
- panel: float32 [32768, 4096], P('rows'), may hold values from -0.09375 to 0.09375
- inv_diag: float32 [4, 1024, 1024], P(None, None, 'rows'), may hold values from -0.075 to 1.4, as said below
Outputs:
- solution: float32 [32768, 1024], P('rows', 'rhs')
Inputs may be any that keep to these rules, and one draw needn't show every extreme that they name: For each rows index a, send_order[a * 256 : (a + 1) * 256] is a permutation of 0 .. 255 whose destinations (as the steps define them) do not fall. Each row and each column of send_count sums to 256; some entry equals 4. There are a permutation p of the rows indices and a table h with send_count[a, p(j)] = h[(j - a) mod 128]. `recv_slot`: every rows index receives each slot 0 .. 255 exactly once. Each inv_diag[k] is lower triangular with diagonal entries from 0.6 to 1.4 and entries below the diagonal within -0.075 to 0.075.
All inputs are finite; a program needn't handle non-finite values.
Results may differ from a plain program's by a relative error of at most 0.0001.
Values sent between devices are 32-bit elements; how exact they have to be, the bound alone decides.
No kernel may reach another device: no remote copies, remote signals or barrier semaphores. Data moves between devices by JAX's collectives and lax.ppermute only.
A program may use at most 64 MiB of HBM per device.

v0:
```python
import jax
import jax.numpy as jnp
from jax import lax
from jax.sharding import Mesh, PartitionSpec as P

ROWS = ("x", "z", "core")
SWAP = [(0, 1), (1, 0)]


def product(left, right, contract=((1,), (0,))):
    return lax.dot_general(
        left,
        right,
        (contract, ((), ())),
        precision=lax.Precision.HIGHEST,
        preferred_element_type=jnp.float32,
    )


def redistribute(targets, send_order, send_count, recv_slot):
    groups = lax.axis_size(ROWS)
    arrived = lax.all_to_all(targets, "rhs", split_axis=1, concat_axis=0, tiled=True)
    rows_local, columns = arrived.shape
    capacity, tag = (4, 64)
    counts = send_count[0]
    dest = jnp.arange(groups, dtype=jnp.int32)
    starts = jnp.sum(jnp.where(dest[None, :] < dest[:, None], counts[None, :], 0), axis=1)
    index = jnp.arange(rows_local, dtype=jnp.int32)
    position = jnp.sum(jnp.where(send_order[:, None] == index[None, :], index[:, None], 0), axis=0)
    slot_number = jnp.arange(capacity, dtype=jnp.int32)
    listed = starts[None, :] + slot_number[:, None]
    listed = jnp.where(slot_number[:, None] < counts[None, :], listed, -1)
    picked = (listed[:, :, None] == position[None, None, :]).astype(jnp.float32)
    picked = picked.reshape(capacity * groups, rows_local)
    landing = jnp.broadcast_to((recv_slot + 1).astype(jnp.float32)[:, None], (rows_local, 2 * tag))
    planes = product(picked, jnp.concatenate([arrived, landing], axis=1))
    planes = planes.reshape(capacity, groups, columns + 2 * tag)
    halves = [
        jnp.concatenate(
            [
                planes[s, :, :columns],
                planes[s + 1, :, :columns],
                planes[s, :, columns : columns + tag],
                planes[s + 1, :, columns : columns + tag],
            ],
            axis=1,
        )
        for s in range(0, capacity, 2)
    ]
    incoming = lax.all_to_all(
        jnp.stack(halves, axis=1), ROWS, split_axis=0, concat_axis=0, tiled=True
    )
    total = 0.0
    for h in range(capacity // 2):
        half = incoming[:, h]
        for s in range(2):
            label = half[:, 2 * columns + s * tag : 2 * columns + s * tag + 1] - 1.0
            placed = (label.astype(jnp.int32) == index[None, :]).astype(jnp.float32)
            rows = half[:, s * columns : (s + 1) * columns]
            total = total + product(placed, rows, ((0,), (0,)))
    return total


def shards(targets, send_order, send_count, recv_slot, panel, inv_diag):
    sections, block_rows, share = inv_diag.shape
    nx, nz, nc = (lax.axis_size(a) for a in ROWS)
    zi = lax.axis_index("z")
    first = lax.axis_index("core") == 0
    even = zi % 2 == 0
    square = sections * share
    inverse_columns = jnp.swapaxes(inv_diag, 1, 2)

    def tile(j, k):
        if j == k:
            return inverse_columns[k]
        return panel[j * share : (j + 1) * share, k * block_rows : (k + 1) * block_rows]

    weight = {}
    early = [(0, 0), (1, 0)]
    late = [(j, k) for j in range(sections) for k in range(j + 1) if (j, k) not in early]
    for names in (early, late):
        gathered = lax.all_gather(jnp.stack([tile(j, k) for j, k in names]), "z")
        for i, name in enumerate(names):
            weight[name] = gathered[:, i].reshape(nz * share, block_rows)
    residual = redistribute(targets, send_order, send_count, recv_slot)
    columns = residual.shape[1] // 2
    halves = jnp.stack([residual[:square, :columns], residual[:square, columns:]])
    tops = jnp.broadcast_to(halves[None], (nz // 2,) + halves.shape).reshape(nz, square, columns)
    tops = lax.all_to_all(tops, "z", split_axis=0, concat_axis=0, tiled=True)
    pending = [
        tops[:, k * share : (k + 1) * share].reshape(nz * share, columns) for k in range(sections)
    ]
    left, right = (residual[square:, :columns], residual[square:, columns:])
    below = [jnp.where(even, left, right), jnp.where(even, right, left)]
    start = ((lax.axis_index("x") * nz + zi) * nc + lax.axis_index("core")) * share
    finished = []
    for k in range(sections):
        partial = product(weight[k, k], pending[k], ((0,), (0,)))
        partial = partial.reshape(nx * nz, nc, share, columns)
        keep = jnp.where(first, partial[:, 0], partial[:, 1])
        give = jnp.where(first, partial[:, 1], partial[:, 0])
        half = keep + lax.ppermute(give, "core", SWAP)
        copies = jnp.broadcast_to(half[None], (nx,) + half.shape)
        mine = jnp.sum(lax.all_to_all(copies, "x", split_axis=0, concat_axis=0, tiled=True), axis=0)
        other = lax.ppermute(mine, "core", SWAP)
        solved = jnp.stack([jnp.where(first, mine, other), jnp.where(first, other, mine)], axis=1)
        solved = solved.reshape(block_rows, columns)
        for j in range(k + 1, sections):
            pending[j] = pending[j] - product(weight[j, k], solved)
        traded = lax.ppermute(solved, "z", [(i, i ^ 1) for i in range(nz)])
        factor = panel[square:, k * block_rows : (k + 1) * block_rows]
        pieces = []
        for h, block in enumerate((solved, traded)):
            below[h] = below[h] - product(factor, block)
            pieces.append(lax.dynamic_slice_in_dim(block, start, share, 0))
        finished.append(pieces)
    ends = [jnp.concatenate([f[h] for f in finished] + [below[h]], axis=0) for h in range(2)]
    return jnp.concatenate(
        [jnp.where(even, ends[0], ends[1]), jnp.where(even, ends[1], ends[0])], axis=1
    )


def solution(mesh):
    ny = mesh.shape["rhs"]
    split = Mesh(mesh.devices.reshape(4, 16, 2, ny), ROWS + ("rhs",))
    placed = (
        P(ROWS + ("rhs",), None),
        P(ROWS),
        P(ROWS, None),
        P(ROWS),
        P(ROWS, None),
        P(None, None, ROWS),
    )
    return jax.shard_map(
        shards, mesh=split, in_specs=placed, out_specs=P(ROWS, "rhs"), check_vma=False
    )
```

profile of v0, /device:TPU:1, one launch (start us, length us, event | category | flops | bytes accessed | tf_op | source)
XLA Modules:
  0.0 300.6 jit_solution(726331077672846849)
XLA Ops:
  14.1 1.7 copy.128
  15.8 5.0 %all-to-all-start = ((f32[64,4,256]{2,0,1:T(8,128)}), f32[64,4,256]{2,0,1:T(8,128)S(1)}, u32[]{:S(2)}, u32[]{:S(2)}) async-start(f32[64,4,256]{2,0,1:T(8,128)} %bitcast.223), calls=%async_computation | async-start | bytes 524288 | tf_op jit(solution)/shard_map/all_to_all | solution.py:22
  23.7 2.6 all-to-all-done
  27.3 1.4 copy.87
  28.7 21.0 %all-to-all-start.1 = ((f32[128,2,640]{2,1,0:T(2,128)}), f32[128,2,640]{2,1,0:T(2,128)S(1)}, u32[]{:S(2)}, u32[]{:S(2)}) async-start(f32[128,2,640]{2,1,0:T(2,128)} %copy.87), calls=%async_computation.1 | async-start | bytes 1310720 | tf_op jit(solution)/shard_map/all_to_all | solution.py:50
  50.4 43.7 %all-to-all-done.1 = f32[128,2,640]{2,1,0:T(2,128)S(1)} async-done(((f32[128,2,640]{2,1,0:T(2,128)}), f32[128,2,640]{2,1,0:T(2,128)S(1)}, u32[]{:S(2)}, u32[]{:S(2)}) %all-to-all-start.1) | async-done | bytes 655392 | tf_op jit(solution)/shard_map/all_to_all | solution.py:50
  97.4 4.1 %all-to-all-start.2 = ((f32[16,32,128]{2,1,0:T(8,128)}), f32[16,32,128]{2,1,0:T(8,128)S(1)}, u32[]{:S(2)}, u32[]{:S(2)}) async-start(f32[16,32,128]{2,1,0:T(8,128)} %bitcast.23), calls=%async_computation.2 | async-start | bytes 524288 | tf_op jit(solution)/shard_map/all_to_all | solution.py:89
  101.5 1.1 slice_bitcast_fusion.15
  102.8 12.3 %all-to-all-done.2 = f32[16,32,128]{2,1,0:T(8,128)S(1)} async-done(((f32[16,32,128]{2,1,0:T(8,128)}), f32[16,32,128]{2,1,0:T(8,128)S(1)}, u32[]{:S(2)}, u32[]{:S(2)}) %all-to-all-start.2) | async-done | bytes 262176 | tf_op jit(solution)/shard_map/all_to_all | solution.py:89
  115.7 7.5 %collective-permute-start = (f32[64,8,128]{2,1,0:T(8,128)S(1)}, f32[64,8,128]{2,1,0:T(8,128)S(1)}, u32[]{:S(2)}, u32[]{:S(2)}) collective-permute-start(f32[64,8,128]{2,1,0:T(8,128)S(1)} %select_bitcast_fusion.11), channel_id=1, source_target_pairs={{0,4},{4,0},{1,5},{5,1},{2,6},{6,2},{3,7},{7,3},{8,12},{12,8},{9,1... | collective-permute-start | bytes 786440 | tf_op jit(solution)/shard_map/ppermute | solution.py:102
  123.2 1.1 collective-permute-done
  124.5 17.7 %all_to_all.49 = f32[4,64,8,128]{3,2,1,0:T(8,128)S(1)} all-to-all(f32[4,64,8,128]{3,2,1,0:T(8,128)S(1)} %broadcast_in_dim.47), channel_id=1, replica_groups=mesh['x'=4,'z'=16,'core'=2,'rhs'=4] {'x'}, dimensions={0} | all-to-all | bytes 2097152 | tf_op jit(solution)/shard_map/all_to_all | solution.py:104
  142.2 3.7 %collective-permute-start.1 = (f32[64,8,128]{2,1,0:T(8,128)S(1)}, f32[64,8,128]{2,1,0:T(8,128)S(1)}, u32[]{:S(2)}, u32[]{:S(2)}) collective-permute-start(f32[64,8,128]{2,1,0:T(8,128)S(1)} %reduce_sum.56), channel_id=1, source_target_pairs={{0,4},{4,0},{1,5},{5,1},{2,6},{6,2},{3,7},{7,3},{8,12},{12,8},{9,1... | collective-permute-start | bytes 786440 | tf_op jit(solution)/shard_map/ppermute | solution.py:105
  145.9 1.1 collective-permute-done.1
  147.9 20.6 %all-gather.7.cloned.1.call-done = f32[128,8,1024]{2,1,0:T(8,128)} async-done(((f32[8,8,1024]{2,1,0:T(8,128)}), f32[128,8,1024]{2,1,0:T(8,128)}) %all-gather.7.cloned.1.call-update) | async-done | bytes 4194320 | tf_op jit(solution)/shard_map/all_gather | solution.py:82
  168.5 1.5 slice_bitcast_fusion.6
  170.8 10.6 %collective-permute-start.2 = (f32[64,8,128]{2,1,0:T(8,128)S(1)}, f32[64,8,128]{2,1,0:T(8,128)S(1)}, u32[]{:S(2)}, u32[]{:S(2)}) collective-permute-start(f32[64,8,128]{2,1,0:T(8,128)S(1)} %select_bitcast_fusion.8), channel_id=1, source_target_pairs={{0,4},{4,0},{1,5},{5,1},{2,6},{6,2},{3,7},{7,3},{8,12},{12,8},{9,1... | collective-permute-start | bytes 786440 | tf_op jit(solution)/shard_map/ppermute | solution.py:102
  181.4 1.1 collective-permute-done.2
  182.6 18.3 %all_to_all.50 = f32[4,64,8,128]{3,2,1,0:T(8,128)S(1)} all-to-all(f32[4,64,8,128]{3,2,1,0:T(8,128)S(1)} %broadcast_in_dim.48), channel_id=1, replica_groups=mesh['x'=4,'z'=16,'core'=2,'rhs'=4] {'x'}, dimensions={0} | all-to-all | bytes 2097152 | tf_op jit(solution)/shard_map/all_to_all | solution.py:104
  201.0 3.7 %collective-permute-start.3 = (f32[64,8,128]{2,1,0:T(8,128)S(1)}, f32[64,8,128]{2,1,0:T(8,128)}, u32[]{:S(2)}, u32[]{:S(2)}) collective-permute-start(f32[64,8,128]{2,1,0:T(8,128)S(1)} %reduce_sum.57), channel_id=1, source_target_pairs={{0,4},{4,0},{1,5},{5,1},{2,6},{6,2},{3,7},{7,3},{8,12},{12,8},{9,1... | collective-permute-start | bytes 786440 | tf_op jit(solution)/shard_map/ppermute | solution.py:105
  204.9 1.7 convolution_subtract_fusion.4
  207.7 1.7 fusion.11
  210.0 2.1 collective-permute-start.4
  212.1 1.3 collective-permute-done.4
  214.5 3.5 %all-to-all-start.5 = ((f32[4,64,8,128]{3,2,1,0:T(8,128)}), f32[4,64,8,128]{3,2,1,0:T(8,128)S(1)}, u32[]{:S(2)}, u32[]{:S(2)}) async-start(f32[4,64,8,128]{3,2,1,0:T(8,128)} %broadcast_in_dim.49), calls=%async_computation.5 | async-start | bytes 2097152 | tf_op jit(solution)/shard_map/all_to_all | solution.py:104
  218.0 3.0 %collective-permute-start.8 = (f32[1024,128]{1,0:T(8,128)S(1)}, f32[1024,128]{1,0:T(8,128)}, u32[]{:S(2)}, u32[]{:S(2)}) collective-permute-start(f32[1024,128]{1,0:T(8,128)S(1)} %bitcast.226), channel_id=1, source_target_pairs={{0,8},{8,0},{16,24},{24,16},{32,40},{40,32},{48,56},{56,48},{64,72... | collective-permute-start | bytes 1572872 | tf_op jit(solution)/shard_map/ppermute | solution.py:110
  221.7 11.4 %all-to-all-done.5 = f32[4,64,8,128]{3,2,1,0:T(8,128)S(1)} async-done(((f32[4,64,8,128]{3,2,1,0:T(8,128)}), f32[4,64,8,128]{3,2,1,0:T(8,128)S(1)}, u32[]{:S(2)}, u32[]{:S(2)}) %all-to-all-start.5) | async-done | bytes 1048608 | tf_op jit(solution)/shard_map/all_to_all | solution.py:104
  233.2 2.9 collective-permute-start.5
  236.0 1.7 convolution_subtract_fusion.2
  237.9 1.7 convolution_subtract_fusion.1
  239.7 1.7 fusion.10
  242.0 1.9 collective-permute-start.6
  244.0 2.1 fusion.5
  246.0 3.0 %collective-permute-start.9 = (f32[1024,128]{1,0:T(8,128)S(1)}, f32[1024,128]{1,0:T(8,128)S(1)}, u32[]{:S(2)}, u32[]{:S(2)}) collective-permute-start(f32[1024,128]{1,0:T(8,128)S(1)} %bitcast.232), channel_id=1, source_target_pairs={{0,8},{8,0},{16,24},{24,16},{32,40},{40,32},{48,56},{56,48},{64,72... | collective-permute-start | bytes 1572872 | tf_op jit(solution)/shard_map/ppermute | solution.py:110
  249.1 1.1 broadcast_in_dim.50
  250.2 3.5 %all-to-all-start.6 = ((f32[4,64,8,128]{3,2,1,0:T(8,128)}), f32[4,64,8,128]{3,2,1,0:T(8,128)S(1)}, u32[]{:S(2)}, u32[]{:S(2)}) async-start(f32[4,64,8,128]{3,2,1,0:T(8,128)} %broadcast_in_dim.50), calls=%async_computation.6 | async-start | bytes 2097152 | tf_op jit(solution)/shard_map/all_to_all | solution.py:104
  253.7 1.3 constant_dynamic-update-slice_fusion.15
  255.6 2.7 fusion.4
  258.3 2.6 collective-permute-done.9
  261.5 2.1 convolution_bitcast_fusion.2
  263.6 3.2 %collective-permute-start.10 = (f32[1024,128]{1,0:T(8,128)S(1)}, f32[1024,128]{1,0:T(8,128)S(1)}, u32[]{:S(2)}, u32[]{:S(2)}) collective-permute-start(f32[1024,128]{1,0:T(8,128)S(1)} %bitcast.236), channel_id=1, source_target_pairs={{0,8},{8,0},{16,24},{24,16},{32,40},{40,32},{48,56},{56,48},{64,72... | collective-permute-start | bytes 1572872 | tf_op jit(solution)/shard_map/ppermute | solution.py:110
  266.8 1.3 all-to-all-done.6
  268.1 3.8 %collective-permute-start.7 = (f32[64,8,128]{2,1,0:T(8,128)S(1)}, f32[64,8,128]{2,1,0:T(8,128)S(1)}, u32[]{:S(2)}, u32[]{:S(2)}) collective-permute-start(f32[64,8,128]{2,1,0:T(8,128)S(1)} %reduce_sum.59), channel_id=1, source_target_pairs={{0,4},{4,0},{1,5},{5,1},{2,6},{6,2},{3,7},{7,3},{8,12},{12,8},{9,1... | collective-permute-start | bytes 786440 | tf_op jit(solution)/shard_map/ppermute | solution.py:105
  272.0 2.1 fusion.3
  274.2 2.3 collective-permute-start.11
  276.5 1.2 collective-permute-done.10
  279.5 10.6 %collective-permute-done.11 = f32[1024,128]{1,0:T(8,128)S(1)} collective-permute-done((f32[1024,128]{1,0:T(8,128)S(1)}, f32[1024,128]{1,0:T(8,128)S(1)}, u32[]{:S(2)}, u32[]{:S(2)}) %collective-permute-start.11) | collective-permute-done | bytes 524320 | tf_op jit(solution)/shard_map/ppermute | solution.py:110
  291.0 1.9 fusion.9
  (100 shorter events, 27.5 us)
Async XLA Ops:
  6.5 95.0 %all-gather.5.cloned.1.call-start = ((), (), s32[]{:S(2)}) async-start(), calls=%async_computation.7 | async-start | bytes 1114112 | tf_op jit(solution)/shard_map/all_gather | solution.py:82
  13.4 15.3 %copy-start.2 = (f32[8,8,1024]{2,1,0:T(8,128)}, f32[8,8,1024]{2,1,0:T(8,128)S(1)}, u32[]{:S(2)}) copy-start(f32[8,8,1024]{2,1,0:T(8,128)S(1)} %get-tuple-element.34) | copy-start | bytes 786436
  15.8 10.5 %all-to-all-start = ((f32[64,4,256]{2,0,1:T(8,128)}), f32[64,4,256]{2,0,1:T(8,128)S(1)}, u32[]{:S(2)}, u32[]{:S(2)}) async-start(f32[64,4,256]{2,0,1:T(8,128)} %bitcast.223), calls=%async_computation | async-start | bytes 524288 | tf_op jit(solution)/shard_map/all_to_all | solution.py:22
  28.7 65.4 %all-to-all-start.1 = ((f32[128,2,640]{2,1,0:T(2,128)}), f32[128,2,640]{2,1,0:T(2,128)S(1)}, u32[]{:S(2)}, u32[]{:S(2)}) async-start(f32[128,2,640]{2,1,0:T(2,128)} %copy.87), calls=%async_computation.1 | async-start | bytes 1310720 | tf_op jit(solution)/shard_map/all_to_all | solution.py:50
  49.7 118.8 %all-gather.7.cloned.1.call-start = ((), (), s32[]{:S(2)}) async-start(), calls=%async_computation.8 | async-start | bytes 4456448 | tf_op jit(solution)/shard_map/all_gather | solution.py:82
  97.4 17.7 %all-to-all-start.2 = ((f32[16,32,128]{2,1,0:T(8,128)}), f32[16,32,128]{2,1,0:T(8,128)S(1)}, u32[]{:S(2)}, u32[]{:S(2)}) async-start(f32[16,32,128]{2,1,0:T(8,128)} %bitcast.23), calls=%async_computation.2 | async-start | bytes 524288 | tf_op jit(solution)/shard_map/all_to_all | solution.py:89
  115.7 8.6 %collective-permute-start = (f32[64,8,128]{2,1,0:T(8,128)S(1)}, f32[64,8,128]{2,1,0:T(8,128)S(1)}, u32[]{:S(2)}, u32[]{:S(2)}) collective-permute-start(f32[64,8,128]{2,1,0:T(8,128)S(1)} %select_bitcast_fusion.11), channel_id=1, source_target_pairs={{0,4},{4,0},{1,5},{5,1},{2,6},{6,2},{3,7},{7,3},{8,12},{12,8},{9,1... | collective-permute-start | bytes 786440 | tf_op jit(solution)/shard_map/ppermute | solution.py:102
  124.4 22.8 %copy-start.1 = (f32[32,8,1024]{2,1,0:T(8,128)S(1)}, f32[32,8,1024]{2,1,0:T(8,128)}, u32[]{:S(2)}) copy-start(f32[32,8,1024]{2,1,0:T(8,128)} %all-gather.5.cloned.1.call-done) | copy-start | bytes 3145732
  142.2 4.8 %collective-permute-start.1 = (f32[64,8,128]{2,1,0:T(8,128)S(1)}, f32[64,8,128]{2,1,0:T(8,128)S(1)}, u32[]{:S(2)}, u32[]{:S(2)}) collective-permute-start(f32[64,8,128]{2,1,0:T(8,128)S(1)} %reduce_sum.56), channel_id=1, source_target_pairs={{0,4},{4,0},{1,5},{5,1},{2,6},{6,2},{3,7},{7,3},{8,12},{12,8},{9,1... | collective-permute-start | bytes 786440 | tf_op jit(solution)/shard_map/ppermute | solution.py:105
  170.8 11.7 %collective-permute-start.2 = (f32[64,8,128]{2,1,0:T(8,128)S(1)}, f32[64,8,128]{2,1,0:T(8,128)S(1)}, u32[]{:S(2)}, u32[]{:S(2)}) collective-permute-start(f32[64,8,128]{2,1,0:T(8,128)S(1)} %select_bitcast_fusion.8), channel_id=1, source_target_pairs={{0,4},{4,0},{1,5},{5,1},{2,6},{6,2},{3,7},{7,3},{8,12},{12,8},{9,1... | collective-permute-start | bytes 786440 | tf_op jit(solution)/shard_map/ppermute | solution.py:102
  201.0 5.6 %collective-permute-start.3 = (f32[64,8,128]{2,1,0:T(8,128)S(1)}, f32[64,8,128]{2,1,0:T(8,128)}, u32[]{:S(2)}, u32[]{:S(2)}) collective-permute-start(f32[64,8,128]{2,1,0:T(8,128)S(1)} %reduce_sum.57), channel_id=1, source_target_pairs={{0,4},{4,0},{1,5},{5,1},{2,6},{6,2},{3,7},{7,3},{8,12},{12,8},{9,1... | collective-permute-start | bytes 786440 | tf_op jit(solution)/shard_map/ppermute | solution.py:105
  210.0 3.4 %collective-permute-start.4 = (f32[64,8,128]{2,1,0:T(8,128)S(1)}, f32[64,8,128]{2,1,0:T(8,128)S(1)}, u32[]{:S(2)}, u32[]{:S(2)}) collective-permute-start(f32[64,8,128]{2,1,0:T(8,128)S(1)} %select_bitcast_fusion.5), channel_id=1, source_target_pairs={{0,4},{4,0},{1,5},{5,1},{2,6},{6,2},{3,7},{7,3},{8,12},{12,8},{9,1... | collective-permute-start | bytes 786440 | tf_op jit(solution)/shard_map/ppermute | solution.py:102
  214.5 18.6 %all-to-all-start.5 = ((f32[4,64,8,128]{3,2,1,0:T(8,128)}), f32[4,64,8,128]{3,2,1,0:T(8,128)S(1)}, u32[]{:S(2)}, u32[]{:S(2)}) async-start(f32[4,64,8,128]{3,2,1,0:T(8,128)} %broadcast_in_dim.49), calls=%async_computation.5 | async-start | bytes 2097152 | tf_op jit(solution)/shard_map/all_to_all | solution.py:104
  218.0 35.7 %collective-permute-start.8 = (f32[1024,128]{1,0:T(8,128)S(1)}, f32[1024,128]{1,0:T(8,128)}, u32[]{:S(2)}, u32[]{:S(2)}) collective-permute-start(f32[1024,128]{1,0:T(8,128)S(1)} %bitcast.226), channel_id=1, source_target_pairs={{0,8},{8,0},{16,24},{24,16},{32,40},{40,32},{48,56},{56,48},{64,72... | collective-permute-start | bytes 1572872 | tf_op jit(solution)/shard_map/ppermute | solution.py:110
  233.2 6.4 %collective-permute-start.5 = (f32[64,8,128]{2,1,0:T(8,128)S(1)}, f32[64,8,128]{2,1,0:T(8,128)S(1)}, u32[]{:S(2)}, u32[]{:S(2)}) collective-permute-start(f32[64,8,128]{2,1,0:T(8,128)S(1)} %reduce_sum.58), channel_id=1, source_target_pairs={{0,4},{4,0},{1,5},{5,1},{2,6},{6,2},{3,7},{7,3},{8,12},{12,8},{9,1... | collective-permute-start | bytes 786440 | tf_op jit(solution)/shard_map/ppermute | solution.py:105
  242.0 7.0 %collective-permute-start.6 = (f32[64,8,128]{2,1,0:T(8,128)S(1)}, f32[64,8,128]{2,1,0:T(8,128)S(1)}, u32[]{:S(2)}, u32[]{:S(2)}) collective-permute-start(f32[64,8,128]{2,1,0:T(8,128)S(1)} %select_bitcast_fusion.2), channel_id=1, source_target_pairs={{0,4},{4,0},{1,5},{5,1},{2,6},{6,2},{3,7},{7,3},{8,12},{12,8},{9,1... | collective-permute-start | bytes 786440 | tf_op jit(solution)/shard_map/ppermute | solution.py:102
  246.0 14.9 %collective-permute-start.9 = (f32[1024,128]{1,0:T(8,128)S(1)}, f32[1024,128]{1,0:T(8,128)S(1)}, u32[]{:S(2)}, u32[]{:S(2)}) collective-permute-start(f32[1024,128]{1,0:T(8,128)S(1)} %bitcast.232), channel_id=1, source_target_pairs={{0,8},{8,0},{16,24},{24,16},{32,40},{40,32},{48,56},{56,48},{64,72... | collective-permute-start | bytes 1572872 | tf_op jit(solution)/shard_map/ppermute | solution.py:110
  250.2 17.9 %all-to-all-start.6 = ((f32[4,64,8,128]{3,2,1,0:T(8,128)}), f32[4,64,8,128]{3,2,1,0:T(8,128)S(1)}, u32[]{:S(2)}, u32[]{:S(2)}) async-start(f32[4,64,8,128]{3,2,1,0:T(8,128)} %broadcast_in_dim.50), calls=%async_computation.6 | async-start | bytes 2097152 | tf_op jit(solution)/shard_map/all_to_all | solution.py:104
  258.3 15.8 %copy-start.3 = (f32[256,128]{1,0:T(8,128)S(1)}, f32[256,128]{1,0:T(8,128)}, u32[]{:S(2)}) copy-start(f32[256,128]{1,0:T(8,128)} %constant_dynamic-update-slice_fusion.10) | copy-start | bytes 393220
  263.6 15.0 %copy-start.4 = (f32[256,128]{1,0:T(8,128)S(1)}, f32[256,128]{1,0:T(8,128)}, u32[]{:S(2)}) copy-start(f32[256,128]{1,0:T(8,128)} %constant_dynamic-update-slice_fusion.14) | copy-start | bytes 393220
  263.6 14.1 %collective-permute-start.10 = (f32[1024,128]{1,0:T(8,128)S(1)}, f32[1024,128]{1,0:T(8,128)S(1)}, u32[]{:S(2)}, u32[]{:S(2)}) collective-permute-start(f32[1024,128]{1,0:T(8,128)S(1)} %bitcast.236), channel_id=1, source_target_pairs={{0,8},{8,0},{16,24},{24,16},{32,40},{40,32},{48,56},{56,48},{64,72... | collective-permute-start | bytes 1572872 | tf_op jit(solution)/shard_map/ppermute | solution.py:110
  268.1 9.6 %copy-start = (f32[256,4096]{1,0:T(8,128)S(1)}, f32[256,4096]{1,0:T(8,128)}, u32[]{:S(2)}) copy-start(f32[256,4096]{1,0:T(8,128)} %param.10) | copy-start | bytes 12582916
  268.1 6.0 %collective-permute-start.7 = (f32[64,8,128]{2,1,0:T(8,128)S(1)}, f32[64,8,128]{2,1,0:T(8,128)S(1)}, u32[]{:S(2)}, u32[]{:S(2)}) collective-permute-start(f32[64,8,128]{2,1,0:T(8,128)S(1)} %reduce_sum.59), channel_id=1, source_target_pairs={{0,4},{4,0},{1,5},{5,1},{2,6},{6,2},{3,7},{7,3},{8,12},{12,8},{9,1... | collective-permute-start | bytes 786440 | tf_op jit(solution)/shard_map/ppermute | solution.py:105
  274.2 15.9 %collective-permute-start.11 = (f32[1024,128]{1,0:T(8,128)S(1)}, f32[1024,128]{1,0:T(8,128)S(1)}, u32[]{:S(2)}, u32[]{:S(2)}) collective-permute-start(f32[1024,128]{1,0:T(8,128)S(1)} %bitcast.245), channel_id=1, source_target_pairs={{0,8},{8,0},{16,24},{24,16},{32,40},{40,32},{48,56},{56,48},{64,72... | collective-permute-start | bytes 1572872 | tf_op jit(solution)/shard_map/ppermute | solution.py:110
Sparse Core Ops, SparseCore 0:
  14.2 78.4 all-gather.4
  94.8 73.6 all-gather.6
where the time goes:
time: 303 us; the launch traced here: 301 us
  waiting for transfers between devices  112 us (37%)
  starting transfers between devices  84.8 us (28%)
  blocking collectives  36 us (12%)
  matrix products  27 us (9%)
  local copies, waits for them, and re-layouts  20.1 us (7%)
  between operations  14.1 us (5%)
  other arithmetic  6.71 us (2%)
    all_to_all x1, waiting for transfers between devices, redistribute(): lax.all_to_all(jnp.stack(halves, axis=1), ROWS, split_axis=0, concat_axis...  43.7 us
    all_to_all x2, blocking collectives, shards(): lax.all_to_all(copies, 'x', split_axis=0, concat_axis=0, tiled=True)  36 us
    dot_general x23, matrix products, product(): lax.dot_general(left, right, (contract, ((), ())), precision=lax.Precisio...  27 us
    ppermute x4, starting transfers between devices, shards(): half = keep + lax.ppermute(give, 'core', SWAP)  22.1 us
    all_to_all x1, starting transfers between devices, redistribute(): lax.all_to_all(jnp.stack(halves, axis=1), ROWS, split_axis=0, concat_axis...  21 us
    all_gather x2, waiting for transfers between devices, shards(): gathered = lax.all_gather(jnp.stack([tile(j, k) for j, k in names]), 'z')  20.7 us
    ppermute x4, waiting for transfers between devices, shards(): traded = lax.ppermute(solved, 'z', [(i, i ^ 1) for i in range(nz)])  14.4 us
    ppermute x4, starting transfers between devices, shards(): other = lax.ppermute(mine, 'core', SWAP)  14.1 us
  transfers between devices with their start and end apart: 19, of which 13 were waited for; matrix products, arithmetic and copies ran while one was open for 12% of the time, Pallas kernels for 0%

commit v1 on v0

--- a/solution.py
+++ b/solution.py
@@ -5,6 +5,31 @@
 
 ROWS = ("x", "z", "core")
 SWAP = [(0, 1), (1, 0)]
+
+
+def do_target(xs, array_axis, block_here):
+    top = xs.shape
+    latest = xs.reshape(
+        *top[:array_axis], block_here, top[array_axis] // block_here, *top[array_axis + 1 :]
+    )
+    return jnp.moveaxis(latest, array_axis, 0)
+
+
+def wait_the_columns(chunk, on_dim):
+    carry_in = list(chunk.shape[1:])
+    carry_in[on_dim] *= chunk.shape[0]
+    return jnp.moveaxis(chunk, 0, on_dim).reshape(carry_in)
+
+
+def _map_ladders(arr_in, link_axis, my_data, original):
+    all_rows, carry = (lax.axis_size(link_axis), lax.axis_index(link_axis))
+    newest = do_target(arr_in, original, all_rows)
+    so_far_all = [newest[carry]]
+    for ii in tuple(range(1, all_rows)):
+        formed = newest[carry ^ ii]
+        so_far_all.append(lax.ppermute(formed, link_axis, [(p, p ^ ii) for p in range(all_rows)]))
+    newest = jnp.stack(so_far_all, axis=0)[carry ^ jnp.arange(all_rows)]
+    return wait_the_columns(newest, my_data)
 
 
 def product(left, right, contract=((1,), (0,))):
@@ -19,7 +44,7 @@
 
 def redistribute(targets, send_order, send_count, recv_slot):
     groups = lax.axis_size(ROWS)
-    arrived = lax.all_to_all(targets, "rhs", split_axis=1, concat_axis=0, tiled=True)
+    arrived = _map_ladders(targets, "rhs", 0, 1)
     rows_local, columns = arrived.shape
     capacity, tag = (4, 64)
     counts = send_count[0]

time: 303 us -> 303 us (level)
  starting transfers between devices: 84.8 us -> 88.9 us
    ppermute x0 -> x3, starting transfers between devices: none -> 9.88 us  [_map_ladders(): lax.ppermute(formed, link_axis, [(p, p ^ ii) for p in range(all_rows)])]
    all_to_all x1 -> x0, starting transfers between devices: 5.01 us -> none  [redistribute(): lax.all_to_all(targets, 'rhs', split_axis=1, concat_axis=0, tiled=True)]
    unnamed x27 -> x31, local copies, waits for them, and re-layouts: 8.48 us -> 8.51 us
  transfers between devices with their start and end apart: 19 -> 21, of which waited for: 13 -> 12; matrix products, arithmetic and copies ran while one was open for 12% -> 12% of each run, Pallas kernels for 0% -> 0%
where the time goes in v1:
time: 303 us; the launch traced here: 301 us
  waiting for transfers between devices  109 us (36%)
  starting transfers between devices  88.9 us (29%)
  blocking collectives  34.2 us (11%)
  matrix products  27 us (9%)
  local copies, waits for them, and re-layouts  20.3 us (7%)
  between operations  14.3 us (5%)
  other arithmetic  6.73 us (2%)
    all_to_all x1, waiting for transfers between devices, redistribute(): lax.all_to_all(jnp.stack(halves, axis=1), ROWS, split_axis=0, concat_axis...  44.1 us
    all_to_all x2, blocking collectives, shards(): lax.all_to_all(copies, 'x', split_axis=0, concat_axis=0, tiled=True)  34.2 us
    dot_general x23, matrix products, product(): lax.dot_general(left, right, (contract, ((), ())), precision=lax.Precisio...  27 us
    ppermute x4, starting transfers between devices, shards(): half = keep + lax.ppermute(give, 'core', SWAP)  21.8 us
    all_to_all x1, starting transfers between devices, redistribute(): lax.all_to_all(jnp.stack(halves, axis=1), ROWS, split_axis=0, concat_axis...  21.1 us
    all_gather x2, waiting for transfers between devices, shards(): gathered = lax.all_gather(jnp.stack([tile(j, k) for j, k in names]), 'z')  19.9 us
    ppermute x4, starting transfers between devices, shards(): other = lax.ppermute(mine, 'core', SWAP)  14.3 us
    ppermute x4, waiting for transfers between devices, shards(): traded = lax.ppermute(solved, 'z', [(i, i ^ 1) for i in range(nz)])  14.2 us
  transfers between devices with their start and end apart: 21, of which 12 were waited for; matrix products, arithmetic and copies ran while one was open for 12% of the time, Pallas kernels for 0%

profile of v1, /device:TPU:1, one launch (start us, length us, event | category | flops | bytes accessed | tf_op | source)
XLA Modules:
  0.0 300.6 jit_solution(14723104141056320887)
XLA Ops:
  14.1 1.1 reshape.142
  15.4 5.5 %collective-permute-start.2 = (f32[64,256]{1,0:T(8,128)S(1)}, f32[64,256]{1,0:T(8,128)S(1)}, u32[]{:S(2)}, u32[]{:S(2)}) collective-permute-start(f32[64,256]{1,0:T(8,128)S(1)} %bitcast.276), channel_id=1, source_target_pairs={{0,3},{1,2},{2,1},{3,0},{4,7},{5,6},{6,5},{7,4},{8,11},{9,10},{10,... | collective-permute-start | bytes 196616 | tf_op jit(solution)/shard_map/ppermute | solution.py:30
  20.9 2.3 collective-permute-start.1
  23.2 2.1 collective-permute-start
  29.9 1.4 copy.82
  31.3 21.1 %all-to-all-start = ((f32[128,2,640]{2,1,0:T(2,128)}), f32[128,2,640]{2,1,0:T(2,128)S(1)}, u32[]{:S(2)}, u32[]{:S(2)}) async-start(f32[128,2,640]{2,1,0:T(2,128)} %copy.82), calls=%async_computation | async-start | bytes 1310720 | tf_op jit(solution)/shard_map/all_to_all | solution.py:75
  53.2 44.1 %all-to-all-done = f32[128,2,640]{2,1,0:T(2,128)S(1)} async-done(((f32[128,2,640]{2,1,0:T(2,128)}), f32[128,2,640]{2,1,0:T(2,128)S(1)}, u32[]{:S(2)}, u32[]{:S(2)}) %all-to-all-start) | async-done | bytes 655392 | tf_op jit(solution)/shard_map/all_to_all | solution.py:75
  100.6 3.5 %all-to-all-start.1 = ((f32[16,32,128]{2,1,0:T(8,128)}), f32[16,32,128]{2,1,0:T(8,128)S(1)}, u32[]{:S(2)}, u32[]{:S(2)}) async-start(f32[16,32,128]{2,1,0:T(8,128)} %bitcast.26), calls=%async_computation.1 | async-start | bytes 524288 | tf_op jit(solution)/shard_map/all_to_all | solution.py:114
  104.2 1.1 slice_bitcast_fusion.15
  105.4 12.4 %all-to-all-done.1 = f32[16,32,128]{2,1,0:T(8,128)S(1)} async-done(((f32[16,32,128]{2,1,0:T(8,128)}), f32[16,32,128]{2,1,0:T(8,128)S(1)}, u32[]{:S(2)}, u32[]{:S(2)}) %all-to-all-start.1) | async-done | bytes 262176 | tf_op jit(solution)/shard_map/all_to_all | solution.py:114
  118.4 7.4 %collective-permute-start.3 = (f32[64,8,128]{2,1,0:T(8,128)S(1)}, f32[64,8,128]{2,1,0:T(8,128)S(1)}, u32[]{:S(2)}, u32[]{:S(2)}) collective-permute-start(f32[64,8,128]{2,1,0:T(8,128)S(1)} %select_bitcast_fusion.11), channel_id=1, source_target_pairs={{0,4},{4,0},{1,5},{5,1},{2,6},{6,2},{3,7},{7,3},{8,12},{12,8},{9,1... | collective-permute-start | bytes 786440 | tf_op jit(solution)/shard_map/ppermute | solution.py:127
  125.8 1.1 collective-permute-done.3
  127.1 17.0 %all_to_all.30 = f32[4,64,8,128]{3,2,1,0:T(8,128)S(1)} all-to-all(f32[4,64,8,128]{3,2,1,0:T(8,128)S(1)} %broadcast_in_dim.47), channel_id=1, replica_groups=mesh['x'=4,'z'=16,'core'=2,'rhs'=4] {'x'}, dimensions={0} | all-to-all | bytes 2097152 | tf_op jit(solution)/shard_map/all_to_all | solution.py:129
  144.2 3.7 %collective-permute-start.4 = (f32[64,8,128]{2,1,0:T(8,128)S(1)}, f32[64,8,128]{2,1,0:T(8,128)S(1)}, u32[]{:S(2)}, u32[]{:S(2)}) collective-permute-start(f32[64,8,128]{2,1,0:T(8,128)S(1)} %reduce_sum.56), channel_id=1, source_target_pairs={{0,4},{4,0},{1,5},{5,1},{2,6},{6,2},{3,7},{7,3},{8,12},{12,8},{9,1... | collective-permute-start | bytes 786440 | tf_op jit(solution)/shard_map/ppermute | solution.py:130
  147.9 1.1 collective-permute-done.4
  149.9 19.9 %all-gather.7.cloned.1.call-done = f32[128,8,1024]{2,1,0:T(8,128)} async-done(((f32[8,8,1024]{2,1,0:T(8,128)}), f32[128,8,1024]{2,1,0:T(8,128)}) %all-gather.7.cloned.1.call-update) | async-done | bytes 4194320 | tf_op jit(solution)/shard_map/all_gather | solution.py:107
  169.8 1.5 slice_bitcast_fusion.6
  172.0 10.5 %collective-permute-start.5 = (f32[64,8,128]{2,1,0:T(8,128)S(1)}, f32[64,8,128]{2,1,0:T(8,128)S(1)}, u32[]{:S(2)}, u32[]{:S(2)}) collective-permute-start(f32[64,8,128]{2,1,0:T(8,128)S(1)} %select_bitcast_fusion.8), channel_id=1, source_target_pairs={{0,4},{4,0},{1,5},{5,1},{2,6},{6,2},{3,7},{7,3},{8,12},{12,8},{9,1... | collective-permute-start | bytes 786440 | tf_op jit(solution)/shard_map/ppermute | solution.py:127
  182.6 1.1 collective-permute-done.5
  183.8 17.2 %all_to_all.31 = f32[4,64,8,128]{3,2,1,0:T(8,128)S(1)} all-to-all(f32[4,64,8,128]{3,2,1,0:T(8,128)S(1)} %broadcast_in_dim.48), channel_id=1, replica_groups=mesh['x'=4,'z'=16,'core'=2,'rhs'=4] {'x'}, dimensions={0} | all-to-all | bytes 2097152 | tf_op jit(solution)/shard_map/all_to_all | solution.py:129
  201.1 3.9 %collective-permute-start.6 = (f32[64,8,128]{2,1,0:T(8,128)S(1)}, f32[64,8,128]{2,1,0:T(8,128)}, u32[]{:S(2)}, u32[]{:S(2)}) collective-permute-start(f32[64,8,128]{2,1,0:T(8,128)S(1)} %reduce_sum.57), channel_id=1, source_target_pairs={{0,4},{4,0},{1,5},{5,1},{2,6},{6,2},{3,7},{7,3},{8,12},{12,8},{9,1... | collective-permute-start | bytes 786440 | tf_op jit(solution)/shard_map/ppermute | solution.py:130
  205.2 1.7 convolution_subtract_fusion.4
  207.9 1.7 fusion.11
  210.2 1.9 collective-permute-start.7
  212.2 1.5 collective-permute-done.7
  214.7 3.5 %all-to-all-start.4 = ((f32[4,64,8,128]{3,2,1,0:T(8,128)}), f32[4,64,8,128]{3,2,1,0:T(8,128)S(1)}, u32[]{:S(2)}, u32[]{:S(2)}) async-start(f32[4,64,8,128]{3,2,1,0:T(8,128)} %broadcast_in_dim.49), calls=%async_computation.4 | async-start | bytes 2097152 | tf_op jit(solution)/shard_map/all_to_all | solution.py:129
  218.3 2.8 collective-permute-start.11
  221.7 11.7 %all-to-all-done.4 = f32[4,64,8,128]{3,2,1,0:T(8,128)S(1)} async-done(((f32[4,64,8,128]{3,2,1,0:T(8,128)}), f32[4,64,8,128]{3,2,1,0:T(8,128)S(1)}, u32[]{:S(2)}, u32[]{:S(2)}) %all-to-all-start.4) | async-done | bytes 1048608 | tf_op jit(solution)/shard_map/all_to_all | solution.py:129
  233.4 2.9 collective-permute-start.8
  236.3 1.7 convolution_subtract_fusion.2
  238.2 1.7 convolution_subtract_fusion.1
  240.0 1.7 fusion.10
  242.3 1.9 collective-permute-start.9
  244.2 2.1 fusion.5
  246.3 2.8 collective-permute-start.12
  249.1 1.0 broadcast_in_dim.50
  250.2 3.5 %all-to-all-start.5 = ((f32[4,64,8,128]{3,2,1,0:T(8,128)}), f32[4,64,8,128]{3,2,1,0:T(8,128)S(1)}, u32[]{:S(2)}, u32[]{:S(2)}) async-start(f32[4,64,8,128]{3,2,1,0:T(8,128)} %broadcast_in_dim.50), calls=%async_computation.5 | async-start | bytes 2097152 | tf_op jit(solution)/shard_map/all_to_all | solution.py:129
  253.7 1.3 constant_dynamic-update-slice_fusion.15
  255.6 2.7 fusion.4
  258.3 2.9 collective-permute-done.12
  261.7 2.1 convolution_bitcast_fusion.2
  263.8 2.9 collective-permute-start.13
  266.7 1.3 all-to-all-done.5
  268.1 3.8 %collective-permute-start.10 = (f32[64,8,128]{2,1,0:T(8,128)S(1)}, f32[64,8,128]{2,1,0:T(8,128)S(1)}, u32[]{:S(2)}, u32[]{:S(2)}) collective-permute-start(f32[64,8,128]{2,1,0:T(8,128)S(1)} %reduce_sum.59), channel_id=1, source_target_pairs={{0,4},{4,0},{1,5},{5,1},{2,6},{6,2},{3,7},{7,3},{8,12},{12,8},{9,1... | collective-permute-start | bytes 786440 | tf_op jit(solution)/shard_map/ppermute | solution.py:130
  272.0 2.1 fusion.3
  274.2 2.7 collective-permute-start.14
  279.8 10.4 %collective-permute-done.14 = f32[1024,128]{1,0:T(8,128)S(1)} collective-permute-done((f32[1024,128]{1,0:T(8,128)S(1)}, f32[1024,128]{1,0:T(8,128)S(1)}, u32[]{:S(2)}, u32[]{:S(2)}) %collective-permute-start.14) | collective-permute-done | bytes 524320 | tf_op jit(solution)/shard_map/ppermute | solution.py:135
  291.0 1.9 fusion.9
  (113 shorter events, 29.3 us)
Async XLA Ops:
  6.5 97.6 %all-gather.5.cloned.1.call-start = ((), (), s32[]{:S(2)}) async-start(), calls=%async_computation.6 | async-start | bytes 1114112 | tf_op jit(solution)/shard_map/all_gather | solution.py:107
  13.4 16.5 %copy-start.2 = (f32[8,8,1024]{2,1,0:T(8,128)}, f32[8,8,1024]{2,1,0:T(8,128)S(1)}, u32[]{:S(2)}) copy-start(f32[8,8,1024]{2,1,0:T(8,128)S(1)} %get-tuple-element.38) | copy-start | bytes 786436
  15.4 12.9 %collective-permute-start.2 = (f32[64,256]{1,0:T(8,128)S(1)}, f32[64,256]{1,0:T(8,128)S(1)}, u32[]{:S(2)}, u32[]{:S(2)}) collective-permute-start(f32[64,256]{1,0:T(8,128)S(1)} %bitcast.276), channel_id=1, source_target_pairs={{0,3},{1,2},{2,1},{3,0},{4,7},{5,6},{6,5},{7,4},{8,11},{9,10},{10,... | collective-permute-start | bytes 196616 | tf_op jit(solution)/shard_map/ppermute | solution.py:30
  20.9 7.4 %collective-permute-start.1 = (f32[64,256]{1,0:T(8,128)S(1)}, f32[64,256]{1,0:T(8,128)S(1)}, u32[]{:S(2)}, u32[]{:S(2)}) collective-permute-start(f32[64,256]{1,0:T(8,128)S(1)} %bitcast.277), channel_id=1, source_target_pairs={{0,2},{1,3},{2,0},{3,1},{4,6},{5,7},{6,4},{7,5},{8,10},{9,11},{10,... | collective-permute-start | bytes 196616 | tf_op jit(solution)/shard_map/ppermute | solution.py:30
  23.2 5.1 %collective-permute-start = (f32[64,256]{1,0:T(8,128)S(1)}, f32[64,256]{1,0:T(8,128)S(1)}, u32[]{:S(2)}, u32[]{:S(2)}) collective-permute-start(f32[64,256]{1,0:T(8,128)S(1)} %bitcast.278), channel_id=1, source_target_pairs={{0,1},{1,0},{2,3},{3,2},{4,5},{5,4},{6,7},{7,6},{8,9},{9,8},{10,11... | collective-permute-start | bytes 196616 | tf_op jit(solution)/shard_map/ppermute | solution.py:30
  31.3 66.0 %all-to-all-start = ((f32[128,2,640]{2,1,0:T(2,128)}), f32[128,2,640]{2,1,0:T(2,128)S(1)}, u32[]{:S(2)}, u32[]{:S(2)}) async-start(f32[128,2,640]{2,1,0:T(2,128)} %copy.82), calls=%async_computation | async-start | bytes 1310720 | tf_op jit(solution)/shard_map/all_to_all | solution.py:75
  52.4 117.3 %all-gather.7.cloned.1.call-start = ((), (), s32[]{:S(2)}) async-start(), calls=%async_computation.7 | async-start | bytes 4456448 | tf_op jit(solution)/shard_map/all_gather | solution.py:107
  100.6 17.2 %all-to-all-start.1 = ((f32[16,32,128]{2,1,0:T(8,128)}), f32[16,32,128]{2,1,0:T(8,128)S(1)}, u32[]{:S(2)}, u32[]{:S(2)}) async-start(f32[16,32,128]{2,1,0:T(8,128)} %bitcast.26), calls=%async_computation.1 | async-start | bytes 524288 | tf_op jit(solution)/shard_map/all_to_all | solution.py:114
  118.4 8.6 %collective-permute-start.3 = (f32[64,8,128]{2,1,0:T(8,128)S(1)}, f32[64,8,128]{2,1,0:T(8,128)S(1)}, u32[]{:S(2)}, u32[]{:S(2)}) collective-permute-start(f32[64,8,128]{2,1,0:T(8,128)S(1)} %select_bitcast_fusion.11), channel_id=1, source_target_pairs={{0,4},{4,0},{1,5},{5,1},{2,6},{6,2},{3,7},{7,3},{8,12},{12,8},{9,1... | collective-permute-start | bytes 786440 | tf_op jit(solution)/shard_map/ppermute | solution.py:127
  127.0 22.2 %copy-start.1 = (f32[32,8,1024]{2,1,0:T(8,128)S(1)}, f32[32,8,1024]{2,1,0:T(8,128)}, u32[]{:S(2)}) copy-start(f32[32,8,1024]{2,1,0:T(8,128)} %all-gather.5.cloned.1.call-done) | copy-start | bytes 3145732
  144.2 4.8 %collective-permute-start.4 = (f32[64,8,128]{2,1,0:T(8,128)S(1)}, f32[64,8,128]{2,1,0:T(8,128)S(1)}, u32[]{:S(2)}, u32[]{:S(2)}) collective-permute-start(f32[64,8,128]{2,1,0:T(8,128)S(1)} %reduce_sum.56), channel_id=1, source_target_pairs={{0,4},{4,0},{1,5},{5,1},{2,6},{6,2},{3,7},{7,3},{8,12},{12,8},{9,1... | collective-permute-start | bytes 786440 | tf_op jit(solution)/shard_map/ppermute | solution.py:130
  172.0 11.7 %collective-permute-start.5 = (f32[64,8,128]{2,1,0:T(8,128)S(1)}, f32[64,8,128]{2,1,0:T(8,128)S(1)}, u32[]{:S(2)}, u32[]{:S(2)}) collective-permute-start(f32[64,8,128]{2,1,0:T(8,128)S(1)} %select_bitcast_fusion.8), channel_id=1, source_target_pairs={{0,4},{4,0},{1,5},{5,1},{2,6},{6,2},{3,7},{7,3},{8,12},{12,8},{9,1... | collective-permute-start | bytes 786440 | tf_op jit(solution)/shard_map/ppermute | solution.py:127
  201.1 5.8 %collective-permute-start.6 = (f32[64,8,128]{2,1,0:T(8,128)S(1)}, f32[64,8,128]{2,1,0:T(8,128)}, u32[]{:S(2)}, u32[]{:S(2)}) collective-permute-start(f32[64,8,128]{2,1,0:T(8,128)S(1)} %reduce_sum.57), channel_id=1, source_target_pairs={{0,4},{4,0},{1,5},{5,1},{2,6},{6,2},{3,7},{7,3},{8,12},{12,8},{9,1... | collective-permute-start | bytes 786440 | tf_op jit(solution)/shard_map/ppermute | solution.py:130
  210.2 3.4 %collective-permute-start.7 = (f32[64,8,128]{2,1,0:T(8,128)S(1)}, f32[64,8,128]{2,1,0:T(8,128)S(1)}, u32[]{:S(2)}, u32[]{:S(2)}) collective-permute-start(f32[64,8,128]{2,1,0:T(8,128)S(1)} %select_bitcast_fusion.5), channel_id=1, source_target_pairs={{0,4},{4,0},{1,5},{5,1},{2,6},{6,2},{3,7},{7,3},{8,12},{12,8},{9,1... | collective-permute-start | bytes 786440 | tf_op jit(solution)/shard_map/ppermute | solution.py:127
  214.7 18.6 %all-to-all-start.4 = ((f32[4,64,8,128]{3,2,1,0:T(8,128)}), f32[4,64,8,128]{3,2,1,0:T(8,128)S(1)}, u32[]{:S(2)}, u32[]{:S(2)}) async-start(f32[4,64,8,128]{3,2,1,0:T(8,128)} %broadcast_in_dim.49), calls=%async_computation.4 | async-start | bytes 2097152 | tf_op jit(solution)/shard_map/all_to_all | solution.py:129
  218.3 35.4 %collective-permute-start.11 = (f32[1024,128]{1,0:T(8,128)S(1)}, f32[1024,128]{1,0:T(8,128)}, u32[]{:S(2)}, u32[]{:S(2)}) collective-permute-start(f32[1024,128]{1,0:T(8,128)S(1)} %bitcast.237), channel_id=1, source_target_pairs={{0,8},{8,0},{16,24},{24,16},{32,40},{40,32},{48,56},{56,48},{64,72... | collective-permute-start | bytes 1572872 | tf_op jit(solution)/shard_map/ppermute | solution.py:135
  233.4 6.4 %collective-permute-start.8 = (f32[64,8,128]{2,1,0:T(8,128)S(1)}, f32[64,8,128]{2,1,0:T(8,128)S(1)}, u32[]{:S(2)}, u32[]{:S(2)}) collective-permute-start(f32[64,8,128]{2,1,0:T(8,128)S(1)} %reduce_sum.58), channel_id=1, source_target_pairs={{0,4},{4,0},{1,5},{5,1},{2,6},{6,2},{3,7},{7,3},{8,12},{12,8},{9,1... | collective-permute-start | bytes 786440 | tf_op jit(solution)/shard_map/ppermute | solution.py:130
  242.3 6.8 %collective-permute-start.9 = (f32[64,8,128]{2,1,0:T(8,128)S(1)}, f32[64,8,128]{2,1,0:T(8,128)S(1)}, u32[]{:S(2)}, u32[]{:S(2)}) collective-permute-start(f32[64,8,128]{2,1,0:T(8,128)S(1)} %select_bitcast_fusion.2), channel_id=1, source_target_pairs={{0,4},{4,0},{1,5},{5,1},{2,6},{6,2},{3,7},{7,3},{8,12},{12,8},{9,1... | collective-permute-start | bytes 786440 | tf_op jit(solution)/shard_map/ppermute | solution.py:127
  246.3 14.9 %collective-permute-start.12 = (f32[1024,128]{1,0:T(8,128)S(1)}, f32[1024,128]{1,0:T(8,128)S(1)}, u32[]{:S(2)}, u32[]{:S(2)}) collective-permute-start(f32[1024,128]{1,0:T(8,128)S(1)} %bitcast.243), channel_id=1, source_target_pairs={{0,8},{8,0},{16,24},{24,16},{32,40},{40,32},{48,56},{56,48},{64,72... | collective-permute-start | bytes 1572872 | tf_op jit(solution)/shard_map/ppermute | solution.py:135
  250.2 17.9 %all-to-all-start.5 = ((f32[4,64,8,128]{3,2,1,0:T(8,128)}), f32[4,64,8,128]{3,2,1,0:T(8,128)S(1)}, u32[]{:S(2)}, u32[]{:S(2)}) async-start(f32[4,64,8,128]{3,2,1,0:T(8,128)} %broadcast_in_dim.50), calls=%async_computation.5 | async-start | bytes 2097152 | tf_op jit(solution)/shard_map/all_to_all | solution.py:129
  258.3 15.8 %copy-start.3 = (f32[256,128]{1,0:T(8,128)S(1)}, f32[256,128]{1,0:T(8,128)}, u32[]{:S(2)}) copy-start(f32[256,128]{1,0:T(8,128)} %constant_dynamic-update-slice_fusion.10) | copy-start | bytes 393220
  263.8 15.0 %copy-start.4 = (f32[256,128]{1,0:T(8,128)S(1)}, f32[256,128]{1,0:T(8,128)}, u32[]{:S(2)}) copy-start(f32[256,128]{1,0:T(8,128)} %constant_dynamic-update-slice_fusion.14) | copy-start | bytes 393220
  263.8 14.1 %collective-permute-start.13 = (f32[1024,128]{1,0:T(8,128)S(1)}, f32[1024,128]{1,0:T(8,128)S(1)}, u32[]{:S(2)}, u32[]{:S(2)}) collective-permute-start(f32[1024,128]{1,0:T(8,128)S(1)} %bitcast.247), channel_id=1, source_target_pairs={{0,8},{8,0},{16,24},{24,16},{32,40},{40,32},{48,56},{56,48},{64,72... | collective-permute-start | bytes 1572872 | tf_op jit(solution)/shard_map/ppermute | solution.py:135
  268.1 9.8 %copy-start = (f32[256,4096]{1,0:T(8,128)S(1)}, f32[256,4096]{1,0:T(8,128)}, u32[]{:S(2)}) copy-start(f32[256,4096]{1,0:T(8,128)} %param.10) | copy-start | bytes 12582916
  268.1 5.9 %collective-permute-start.10 = (f32[64,8,128]{2,1,0:T(8,128)S(1)}, f32[64,8,128]{2,1,0:T(8,128)S(1)}, u32[]{:S(2)}, u32[]{:S(2)}) collective-permute-start(f32[64,8,128]{2,1,0:T(8,128)S(1)} %reduce_sum.59), channel_id=1, source_target_pairs={{0,4},{4,0},{1,5},{5,1},{2,6},{6,2},{3,7},{7,3},{8,12},{12,8},{9,1... | collective-permute-start | bytes 786440 | tf_op jit(solution)/shard_map/ppermute | solution.py:130
  274.2 15.9 %collective-permute-start.14 = (f32[1024,128]{1,0:T(8,128)S(1)}, f32[1024,128]{1,0:T(8,128)S(1)}, u32[]{:S(2)}, u32[]{:S(2)}) collective-permute-start(f32[1024,128]{1,0:T(8,128)S(1)} %bitcast.256), channel_id=1, source_target_pairs={{0,8},{8,0},{16,24},{24,16},{32,40},{40,32},{48,56},{56,48},{64,72... | collective-permute-start | bytes 1572872 | tf_op jit(solution)/shard_map/ppermute | solution.py:135
Sparse Core Ops, SparseCore 0:
  14.2 78.9 all-gather.4
  95.2 74.4 all-gather.6
